TPU v7x, 32 devices: a whole 2x2x4 slice. The times are simulated.
32 devices in a mesh: dp: 8 (over z, x), ctx: 4 (over y, core).
Axes of the slice: x: 2, y: 2, z: 4, core: 2. Of those that a mesh axis runs over, the one named last changes fastest.
Arguments:
- inputs: bfloat16 [8, 512, 2048], P('dp', 'ctx'), may hold values from -8 to 8
- doc_ids: int32 [8, 512], P('dp', 'ctx'), may hold values from 0 to 3, never falling along the last dimension, each value on 1 to 256 neighbouring positions
- dilation: int32 [1], replicated, may hold values from 1 to 256
- filter_w: bfloat16 [2, 2048, 2048], P(None, 'dp', 'ctx'), may hold values from -0.09375 to 0.09375
- gate_w: bfloat16 [2, 2048, 2048], P(None, 'dp', 'ctx'), may hold values from -0.09375 to 0.09375
- filter_m: float32 [2, 2048, 2048], P(None, 'dp', 'ctx'), may hold values from -0.01171875 to 0.01171875
- filter_v: float32 [2, 2048, 2048], P(None, 'dp', 'ctx'), may hold values from 1e-07 to 4e-06
- gate_m: float32 [2, 2048, 2048], P(None, 'dp', 'ctx'), may hold values from -0.01171875 to 0.01171875
- gate_v: float32 [2, 2048, 2048], P(None, 'dp', 'ctx'), may hold values from 1e-07 to 4e-06
- cotangent: bfloat16 [8, 512, 2048], P('dp', 'ctx'), may hold values from -6 to 6
Outputs:
- layer_out: bfloat16 [8, 512, 2048], P('dp', 'ctx')
- input_grad: bfloat16 [8, 512, 2048], P('dp', 'ctx')
- new_filter_w: bfloat16 [2, 2048, 2048], P(None, 'dp', 'ctx')
- new_gate_w: bfloat16 [2, 2048, 2048], P(None, 'dp', 'ctx')
- new_filter_m: float32 [2, 2048, 2048], P(None, 'dp', 'ctx')
- new_filter_v: float32 [2, 2048, 2048], P(None, 'dp', 'ctx')
- new_gate_m: float32 [2, 2048, 2048], P(None, 'dp', 'ctx')
- new_gate_v: float32 [2, 2048, 2048], P(None, 'dp', 'ctx')
Inputs may be any that keep to these rules, and one draw needn't show every extreme that they name: `doc_ids`: document numbers never fall along a sequence; a document covers at most 256 positions.
All inputs are finite; a program needn't handle non-finite values.
Results may differ from a plain program's by a relative error of at most 0.0075.
Values may be sent and summed in bfloat16 or wider, within the bound.
No kernel may reach another device: no remote copies, remote signals or barrier semaphores. Data moves between devices by JAX's collectives and lax.ppermute only.
A program may use at most 128 MiB of HBM per device.

v0:
```python
import jax
import jax.numpy as jnp
from jax import lax
from jax.sharding import PartitionSpec as P

STEP = 10
BETA_ONE = 0.9
BETA_TWO = 0.95
LEARN_RATE = 0.001
EPSILON = 1e-08


def lagged_rows(sequence, seq_ids, shift_by):
    length = sequence.shape[0]
    start_row = length - shift_by
    padded = jnp.concatenate([jnp.zeros_like(sequence), sequence], axis=0)
    shifted = lax.dynamic_slice_in_dim(padded, start_row, length, 0)
    id_padded = jnp.concatenate([jnp.full((length,), -1, jnp.int32), seq_ids], axis=0)
    id_shifted = lax.dynamic_slice_in_dim(id_padded, start_row, length, 0)
    return jnp.where((id_shifted == seq_ids)[:, None], shifted, jnp.zeros_like(shifted))


def adam_update(weight, moment, second, gradient):
    new_moment = BETA_ONE * moment + (1.0 - BETA_ONE) * gradient
    new_second = BETA_TWO * second + (1.0 - BETA_TWO) * gradient * gradient
    first_fix = 1.0 - BETA_ONE**STEP
    second_fix = 1.0 - BETA_TWO**STEP
    step_size = new_moment / first_fix / (jnp.sqrt(new_second / second_fix) + EPSILON)
    new_weight = (weight.astype(jnp.float32) - LEARN_RATE * step_size).astype(jnp.bfloat16)
    return (new_weight, new_moment, new_second)


def per_device(
    inputs, doc_ids, dilation, filter_w, gate_w, filter_m, filter_v, gate_m, gate_v, cotangent
):
    gathered, gathered_ids = (
        lax.all_gather(inputs, "ctx", axis=1, tiled=True),
        lax.all_gather(doc_ids, "ctx", axis=1, tiled=True),
    )
    sequence = gathered[0]
    seq_ids = gathered_ids[0]
    shift_by = dilation[0]
    lagged = lagged_rows(sequence, seq_ids, shift_by)
    length = sequence.shape[0]
    columns = filter_w.shape[2]
    part_filter = lax.all_gather(filter_w, "dp", axis=1, tiled=True)
    part_gate = lax.all_gather(gate_w, "dp", axis=1, tiled=True)
    seq_cols = sequence
    lag_cols = lagged
    zero_part = jnp.concatenate([part_filter[0], part_gate[0]], axis=1)
    one_part = jnp.concatenate([part_filter[1], part_gate[1]], axis=1)
    pre_act = jnp.dot(seq_cols, zero_part, preferred_element_type=jnp.float32) + jnp.dot(
        lag_cols, one_part, preferred_element_type=jnp.float32
    )
    filter_tanh = jnp.tanh(pre_act[:, :columns])
    gate_sigmoid = jax.nn.sigmoid(pre_act[:, columns:])
    gated_cols = (filter_tanh * gate_sigmoid).astype(jnp.bfloat16)
    gated_rows = lax.all_to_all(gated_cols, "ctx", split_axis=0, concat_axis=1, tiled=True)
    layer_out = (inputs[0].astype(jnp.float32) + gated_rows.astype(jnp.float32)).astype(
        jnp.bfloat16
    )
    cot_cols = lax.all_to_all(cotangent[0], "ctx", split_axis=1, concat_axis=0, tiled=True)
    cot_float = cot_cols.astype(jnp.float32)
    filter_delta = (cot_float * gate_sigmoid * (1.0 - filter_tanh * filter_tanh)).astype(
        jnp.bfloat16
    )
    gate_delta = (cot_float * filter_tanh * gate_sigmoid * (1.0 - gate_sigmoid)).astype(
        jnp.bfloat16
    )
    pre_grad = jnp.concatenate([filter_delta, gate_delta], axis=1)
    back_filter, back_gate = (
        lax.all_gather(filter_w, "dp", axis=1, tiled=True),
        lax.all_gather(gate_w, "dp", axis=1, tiled=True),
    )
    back_zero = jnp.concatenate([back_filter[0], back_gate[0]], axis=1)
    back_one = jnp.concatenate([back_filter[1], back_gate[1]], axis=1)
    ahead_grad = jnp.concatenate([pre_grad, jnp.zeros_like(pre_grad)], axis=0)
    ahead_ids = jnp.concatenate([seq_ids, jnp.full((length,), -1, jnp.int32)], axis=0)
    row_count = cotangent.shape[1] * lax.axis_size("ctx")
    rows_ahead = lax.dynamic_slice_in_dim(ahead_grad, shift_by, row_count, 0)
    ids_later = lax.dynamic_slice_in_dim(ahead_ids, shift_by, row_count, 0)
    near_term = lax.dot_general(
        pre_grad, back_zero, (((1,), (1,)), ((), ())), preferred_element_type=jnp.float32
    )
    far_term = lax.dot_general(
        rows_ahead, back_one, (((1,), (1,)), ((), ())), preferred_element_type=jnp.float32
    )
    input_sum = lax.psum_scatter(
        (
            near_term
            + jnp.where((ids_later == seq_ids)[:, None], far_term, jnp.zeros_like(far_term))
        ).astype(jnp.bfloat16),
        "ctx",
        scatter_dimension=0,
        tiled=True,
    ).astype(jnp.float32)
    input_grad = (cotangent[0].astype(jnp.float32) + input_sum).astype(jnp.bfloat16)
    seq_cols = sequence
    lag_cols = lagged
    grad_zero = lax.dot_general(
        seq_cols, pre_grad, (((0,), (0,)), ((), ())), preferred_element_type=jnp.float32
    )
    grad_one = lax.dot_general(
        lag_cols, pre_grad, (((0,), (0,)), ((), ())), preferred_element_type=jnp.float32
    )
    summed = lax.psum_scatter(
        jnp.stack([grad_zero, grad_one], axis=1), "dp", scatter_dimension=0, tiled=True
    )
    tokens_all = length * lax.axis_size("dp")
    filter_grad = jnp.transpose(summed[:, :, :columns], (1, 0, 2)) / tokens_all
    gate_grad = jnp.transpose(summed[:, :, columns:], (1, 0, 2)) / tokens_all
    new_filter_w, new_filter_m, new_filter_v = adam_update(
        filter_w, filter_m, filter_v, filter_grad
    )
    new_gate_w, new_gate_m, new_gate_v = adam_update(gate_w, gate_m, gate_v, gate_grad)
    return (
        layer_out[None],
        input_grad[None],
        new_filter_w,
        new_gate_w,
        new_filter_m,
        new_filter_v,
        new_gate_m,
        new_gate_v,
    )


def solution(mesh):
    placed = (
        P("dp", "ctx", None),
        P("dp", "ctx"),
        P(),
        P(None, "dp", "ctx"),
        P(None, "dp", "ctx"),
        P(None, "dp", "ctx"),
        P(None, "dp", "ctx"),
        P(None, "dp", "ctx"),
        P(None, "dp", "ctx"),
        P("dp", "ctx", None),
    )
    return jax.shard_map(
        per_device,
        mesh=mesh,
        in_specs=placed,
        out_specs=(
            P("dp", "ctx", None),
            P("dp", "ctx", None),
            P(None, "dp", "ctx"),
            P(None, "dp", "ctx"),
            P(None, "dp", "ctx"),
            P(None, "dp", "ctx"),
            P(None, "dp", "ctx"),
            P(None, "dp", "ctx"),
        ),
        check_vma=False,
    )
```

profile of v0, /device:TPU:0, one launch (start us, length us, event | category | flops | bytes accessed | tf_op | source)
XLA Modules:
  0.0 541.8 jit_solution(2864115587601302465)
XLA Ops:
  11.7 4.3 all-to-all-start.1
  16.7 9.1 %all_gather.17 = s32[1,512]{1,0:T(1,128)S(1)} all-gather(s32[1,128]{1,0:T(1,128)S(1)} %copy-done.17), channel_id=1, replica_groups=mesh['dp'=8,'ctx'=4] {'ctx'}, dimensions={1}, use_global_device_ids=true | all-gather | bytes 2560 | tf_op jit(solution)/shard_map/all_gather | solution.py:38
  25.8 59.9 %all-gather.6.cloned.1.call-done = bf16[2,2048,512]{2,1,0:T(8,128)(2,1)} async-done(((bf16[2,256,512]{2,1,0:T(8,128)(2,1)}), bf16[2,2048,512]{2,1,0:T(8,128)(2,1)}) %all-gather.6.cloned.1.call-update) | async-done | bytes 4194320 | tf_op jit(solution)/shard_map/all_gather | solution.py:47
  85.7 3.8 slice_bitcast_fusion.2
  89.5 69.7 %all-gather.4.cloned.1.call-done = bf16[2,2048,512]{2,1,0:T(8,128)(2,1)} async-done(((bf16[2,256,512]{2,1,0:T(8,128)(2,1)}), bf16[2,2048,512]{2,1,0:T(8,128)(2,1)}) %all-gather.4.cloned.1.call-update) | async-done | bytes 4194320 | tf_op jit(solution)/shard_map/all_gather | solution.py:46
  159.2 4.5 slice_bitcast_fusion.3
  163.7 18.2 %all-gather.8.cloned.1.call-done = bf16[1,512,2048]{2,1,0:T(8,128)(2,1)} async-done(((bf16[1,128,2048]{2,1,0:T(8,128)(2,1)}), bf16[1,512,2048]{2,1,0:T(8,128)(2,1)}) %all-gather.8.cloned.1.call-update) | async-done | bytes 2097168 | tf_op jit(solution)/shard_map/all_gather | solution.py:37
  181.9 4.6 fusion
  186.6 2.3 bitcast_add_fusion
  191.4 2.4 fusion.1
  195.4 3.8 add_convert_fusion
  200.2 2.6 convolution_bitcast_fusion
  202.8 2.4 convolution_bitcast_fusion.1
  205.2 6.2 %pad_maximum_fusion = f32[2048,2,1024]{0,2,1:T(8,128)} fusion(f32[2048,1,1024]{0,2,1:T(8,128)S(1)} %convolution_bitcast_fusion, f32[2048,1,1024]{0,2,1:T(8,128)S(1)} %convolution_bitcast_fusion.1), kind=kLoop, calls=%fused_computation | loop fusion | flops 4194304 | bytes 33554432 | tf_op jit(solution)/shard_map/stack | solution.py:107
  211.4 4.5 all-to-all-start
  220.2 2.5 copy.21
  222.7 7.7 %all-to-all-done = bf16[4,128,512]{2,1,0:T(8,128)(2,1)} async-done(((bf16[4,128,512]{2,1,0:T(8,128)(2,1)}), bf16[4,128,512]{2,1,0:T(8,128)(2,1)}, u32[]{:S(2)}, u32[]{:S(2)}) %all-to-all-start) | async-done | bytes 524320 | tf_op jit(solution)/shard_map/all_to_all | solution.py:58
  233.3 2.9 reshape.41
  236.2 2.3 add_convert_fusion.1
  238.5 2.1 fusion.13
  240.6 279.5 %reduce-scatter.5.cloned.1.call-done = f32[256,2,1024]{0,2,1:T(8,128)} async-done(((f32[2048,2,1024]{0,2,1:T(8,128)}), f32[256,2,1024]{0,2,1:T(8,128)}) %reduce-scatter.5.cloned.1.call-update) | async-done | bytes 2097168 | tf_op jit(solution)/shard_map/reduce_scatter | solution.py:106
  520.1 5.7 %subtract_convert_fusion = (bf16[2,256,512]{1,2,0:T(8,128)(2,1)}, f32[2,256,512]{1,2,0:T(8,128)}, f32[2,256,512]{1,2,0:T(8,128)}, bf16[2,256,512]{1,2,0:T(8,128)...) fusion(bf16[2,256,512]{1,2,0:T(8,128)(2,1)} %copy.24, f32[256,2,1024]{0,2,1:T(8,128)} %reduce-scatter.5.cloned.1.call-done, ...), kind=kLoop, calls=%fused_computation.37 | loop fusion | flops 8388608 | bytes 12582912 | tf_op jit(solution)/shard_map/convert_element_type | solution.py:29
  525.8 2.2 copy.27
  528.0 2.0 copy.28
  (68 shorter events, 21.9 us)
Async XLA Ops:
  7.2 78.5 %all-gather.6.cloned.1.call-start = ((), (), s32[]{:S(2)}) async-start(), calls=%async_computation.5 | async-start | bytes 4718592 | tf_op jit(solution)/shard_map/all_gather | solution.py:47
  7.9 8.7 %copy-start.17 = (s32[1,128]{1,0:T(1,128)S(1)}, s32[1,128]{1,0:T(1,128)}, u32[]{:S(2)}) copy-start(s32[1,128]{1,0:T(1,128)} %param.11) | copy-start | bytes 1540
  7.9 151.3 %all-gather.4.cloned.1.call-start = ((), (), s32[]{:S(2)}) async-start(), calls=%async_computation.4 | async-start | bytes 4718592 | tf_op jit(solution)/shard_map/all_gather | solution.py:46
  8.7 173.3 %all-gather.8.cloned.1.call-start = ((), (), s32[]{:S(2)}) async-start(), calls=%async_computation.6 | async-start | bytes 2621440 | tf_op jit(solution)/shard_map/all_gather | solution.py:37
  11.7 177.2 %all-to-all-start.1 = ((bf16[128,4,512]{2,0,1:T(8,128)(2,1)}), bf16[128,4,512]{2,0,1:T(8,128)(2,1)S(1)}, u32[]{:S(2)}, u32[]{:S(2)}) async-start(bf16[128,4,512]{2,0,1:T(8,128)(2,1)} %copy.19), calls=%async_computation.1 | async-start | bytes 1048576 | tf_op jit(solution)/shard_map/all_to_all | solution.py:62
  16.0 222.5 %reduce-scatter.3.cloned.1.call-start = ((), (), s32[]{:S(2)}) async-start(), calls=%async_computation.7 | async-start | bytes 2621440 | tf_op jit(solution)/shard_map/reduce_scatter | solution.py:88
  89.5 92.4 %copy-start.6 = (bf16[2048,512]{1,0:T(8,128)(2,1)}, bf16[2048,512]{1,0:T(8,128)(2,1)S(1)}, u32[]{:S(2)}) copy-start(bf16[2048,512]{1,0:T(8,128)(2,1)S(1)} %get-tuple-element.25) | copy-start | bytes 6291460
  181.9 4.6 copy-start.8
  181.9 4.6 copy-start.11
  181.9 4.6 copy-start.18
  188.9 2.5 copy-start.12
  190.3 3.4 copy-start.13
  191.4 2.5 copy-start.10
  195.4 4.1 copy-start.19
  199.2 320.9 %reduce-scatter.5.cloned.1.call-start = ((), (), s32[]{:S(2)}) async-start(), calls=%async_computation.8 | async-start | bytes 18874368 | tf_op jit(solution)/shard_map/reduce_scatter | solution.py:106
  211.4 4.6 copy-start.4
  211.4 5.6 %copy-start.5 = (bf16[2,256,512]{2,1,0:T(8,128)(2,1)S(1)}, bf16[2,256,512]{2,1,0:T(8,128)(2,1)}, u32[]{:S(2)}) copy-start(bf16[2,256,512]{2,1,0:T(8,128)(2,1)} %param.13) | copy-start | bytes 1572868
  211.4 6.6 %copy-start.15 = (f32[2,256,512]{2,1,0:T(8,128)S(1)}, f32[2,256,512]{2,1,0:T(8,128)}, u32[]{:S(2)}) copy-start(f32[2,256,512]{2,1,0:T(8,128)} %param.17) | copy-start | bytes 3145732
  211.4 19.1 %all-to-all-start = ((bf16[4,128,512]{2,1,0:T(8,128)(2,1)}), bf16[4,128,512]{2,1,0:T(8,128)(2,1)}, u32[]{:S(2)}, u32[]{:S(2)}) async-start(bf16[4,128,512]{2,1,0:T(8,128)(2,1)} %bitcast.8), calls=%async_computation | async-start | bytes 1048576 | tf_op jit(solution)/shard_map/all_to_all | solution.py:58
  215.9 2.4 copy-start.16
  525.8 4.2 copy-start.3
  525.8 5.6 %copy-start.2 = (f32[2,256,512]{1,2,0:T(8,128)S(1)}, f32[2,256,512]{1,2,0:T(8,128)}, u32[]{:S(2)}) copy-start(f32[2,256,512]{1,2,0:T(8,128)} %get-tuple-element.29) | copy-start | bytes 3145732
  530.0 2.6 copy-start.1
  531.3 2.6 copy-start
  (3 other events, 4.2 us)
Sparse Core Ops, SparseCore 0:
  10.2 75.4 all-gather.5
  87.9 71.2 all-gather.3
  160.8 21.0 all-gather.7
  199.3 36.7 reduce-scatter.2
  239.8 280.2 reduce-scatter.4
where the time goes:
time: 542 us
  waiting for transfers between devices  437 us (81%)
  local copies, waits for them, and re-layouts  34.8 us (6%)
  other arithmetic  19 us (4%)
  matrix products  18.1 us (3%)
  between operations  14.7 us (3%)
  starting transfers between devices  9.11 us (2%)
  blocking collectives  9.06 us (2%)
    reduce_scatter x1, waiting for transfers between devices, per_device(): lax.psum_scatter(jnp.stack([grad_zero, grad_one], axis=1), 'dp', scatter_...  279 us
    all_gather x1, waiting for transfers between devices, per_device(): part_filter = lax.all_gather(filter_w, 'dp', axis=1, tiled=True)  69.7 us
    all_gather x1, waiting for transfers between devices, per_device(): part_gate = lax.all_gather(gate_w, 'dp', axis=1, tiled=True)  59.9 us
    unnamed x52, local copies, waits for them, and re-layouts  19.5 us
    all_gather x1, waiting for transfers between devices, per_device(): lax.all_gather(inputs, 'ctx', axis=1, tiled=True)  18.2 us
  transfers between devices with their start and end apart: 7, of which 5 were waited for; matrix products, arithmetic and copies ran while one was open for 8% of the time, Pallas kernels for 0%

commit v1 on v0

--- a/solution.py
+++ b/solution.py
@@ -8,6 +8,28 @@
 BETA_TWO = 0.95
 LEARN_RATE = 0.001
 EPSILON = 1e-08
+
+
+def joined_along(tiles, dim):
+    shape = list(tiles.shape[1:])
+    shape[dim] *= tiles.shape[0]
+    return jnp.moveaxis(tiles, 0, dim).reshape(shape)
+
+
+def ring_gather(x, axis, dim):
+    size = lax.axis_size(axis)
+    pairs = [(i, (i + 1) % size) for i in range(size)]
+    back = [(b, a) for a, b in pairs]
+    lower, upper = ([], [])
+    for step in range(size - 1):
+        if step % 2 == 0:
+            lower.append(lax.ppermute(lower[-1] if lower else x, axis, pairs))
+        else:
+            upper.append(lax.ppermute(upper[-1] if upper else x, axis, back))
+    blocks = jnp.stack([*lower[::-1], x, *upper])
+    shift = lax.axis_index(axis) - len(lower)
+    blocks = blocks[(jnp.arange(size) - shift) % size]
+    return joined_along(blocks, dim)
 
 
 def lagged_rows(sequence, seq_ids, shift_by):
@@ -44,7 +66,7 @@
     length = sequence.shape[0]
     columns = filter_w.shape[2]
     part_filter = lax.all_gather(filter_w, "dp", axis=1, tiled=True)
-    part_gate = lax.all_gather(gate_w, "dp", axis=1, tiled=True)
+    part_gate = ring_gather(gate_w, "dp", 1)
     seq_cols = sequence
     lag_cols = lagged
     zero_part = jnp.concatenate([part_filter[0], part_gate[0]], axis=1)

time: 542 us -> 585 us (1.079)
  local copies, waits for them, and re-layouts: 34.8 us -> 51.1 us
  starting transfers between devices: 9.11 us -> 25.4 us
  waiting for transfers between devices: 437 us -> 445 us
    ppermute x0 -> x7, waiting for transfers between devices: none -> 72.9 us  [the longest x4 71.9 us: ring_gather(): lower.append(lax.ppermute(lower[-1] if lower else x, axis, pairs))]
    all_gather x1, waiting for transfers between devices: 69.7 us -> 0.88 us  [per_device(): part_filter = lax.all_gather(filter_w, 'dp', axis=1, tiled=True)]
    ppermute x0 -> x7, starting transfers between devices: none -> 17.2 us  [the longest x3 11.2 us: ring_gather(): upper.append(lax.ppermute(upper[-1] if upper else x, axis, back))]
    unnamed x52 -> x61, local copies, waits for them, and re-layouts: 19.5 us -> 27.5 us
  transfers between devices with their start and end apart: 7 -> 14, of which waited for: 5 -> 10; matrix products, arithmetic and copies ran while one was open for 8% -> 11% of each run, Pallas kernels for 0% -> 0%
where the time goes in v1:
time: 585 us
  waiting for transfers between devices  445 us (76%)
  local copies, waits for them, and re-layouts  51.1 us (9%)
  starting transfers between devices  25.4 us (4%)
  other arithmetic  19.9 us (3%)
  matrix products  19.7 us (3%)
  between operations  14.7 us (3%)
  blocking collectives  8.98 us (2%)
    reduce_scatter x1, waiting for transfers between devices, per_device(): lax.psum_scatter(jnp.stack([grad_zero, grad_one], axis=1), 'dp', scatter_...  277 us
    ppermute x4, waiting for transfers between devices, ring_gather(): lower.append(lax.ppermute(lower[-1] if lower else x, axis, pairs))  71.9 us
    all_gather x1, waiting for transfers between devices, per_device(): lax.all_gather(gate_w, 'dp', axis=1, tiled=True)  64.6 us
    unnamed x61, local copies, waits for them, and re-layouts  27.5 us
    all_gather x1, waiting for transfers between devices, per_device(): lax.all_gather(inputs, 'ctx', axis=1, tiled=True)  19.2 us
  transfers between devices with their start and end apart: 14, of which 10 were waited for; matrix products, arithmetic and copies ran while one was open for 11% of the time, Pallas kernels for 0%

profile of v1, /device:TPU:0, one launch (start us, length us, event | category | flops | bytes accessed | tf_op | source)
XLA Modules:
  0.0 584.6 jit_solution(14832088534337028818)
XLA Ops:
  9.4 3.0 collective-permute-start
  12.4 16.8 %collective-permute-done = bf16[2,256,512]{2,1,0:T(8,128)(2,1)S(1)} collective-permute-done((bf16[2,256,512]{2,1,0:T(8,128)(2,1)}, bf16[2,256,512]{2,1,0:T(8,128)(2,1)S(1)}, u32[]{:S(2)}, u32[]{:S(2)}) %collective-permute-start) | collective-permute-done | bytes 524320 | tf_op jit(solution)/shard_map/ppermute | solution.py:26
  29.7 4.3 collective-permute-start.4
  34.0 21.8 %collective-permute-done.1 = bf16[2,256,512]{2,1,0:T(8,128)(2,1)S(1)} collective-permute-done((bf16[2,256,512]{2,1,0:T(8,128)(2,1)S(1)}, bf16[2,256,512]{2,1,0:T(8,128)(2,1)S(1)}, u32[]{:S(2)}, u32[]{:S(2)}) %collective-permute-start.1) | collective-permute-done | bytes 524320 | tf_op jit(solution)/shard_map/ppermute | solution.py:26
  55.8 4.7 collective-permute-start.5
  60.5 27.2 %collective-permute-done.2 = bf16[2,256,512]{2,1,0:T(8,128)(2,1)} collective-permute-done((bf16[2,256,512]{2,1,0:T(8,128)(2,1)S(1)}, bf16[2,256,512]{2,1,0:T(8,128)(2,1)}, u32[]{:S(2)}, u32[]{:S(2)}) %collective-permute-start.2) | collective-permute-done | bytes 524320 | tf_op jit(solution)/shard_map/ppermute | solution.py:26
  87.7 2.6 collective-permute-start.3
  92.6 3.5 all-to-all-start.1
  96.8 9.0 %all_gather.15 = s32[1,512]{1,0:T(1,128)S(1)} all-gather(s32[1,128]{1,0:T(1,128)S(1)} %copy-done.18), channel_id=1, replica_groups=mesh['dp'=8,'ctx'=4] {'ctx'}, dimensions={1}, use_global_device_ids=true | all-gather | bytes 2560 | tf_op jit(solution)/shard_map/all_gather | solution.py:60
  108.0 6.1 %collective-permute-done.3 = bf16[2,256,512]{2,1,0:T(8,128)(2,1)} collective-permute-done((bf16[2,256,512]{2,1,0:T(8,128)(2,1)}, bf16[2,256,512]{2,1,0:T(8,128)(2,1)}, u32[]{:S(2)}, u32[]{:S(2)}) %collective-permute-start.3) | collective-permute-done | bytes 524320 | tf_op jit(solution)/shard_map/ppermute | solution.py:26
  125.0 4.9 gather_fusion
  129.9 4.6 fusion.37
  135.3 3.8 slice_bitcast_fusion.3
  139.2 19.2 %all-gather.6.cloned.1.call-done = bf16[1,512,2048]{2,1,0:T(8,128)(2,1)} async-done(((bf16[1,128,2048]{2,1,0:T(8,128)(2,1)}), bf16[1,512,2048]{2,1,0:T(8,128)(2,1)}) %all-gather.6.cloned.1.call-update) | async-done | bytes 2097168 | tf_op jit(solution)/shard_map/all_gather | solution.py:59
  158.3 4.6 fusion
  168.8 64.6 %all-gather.8.cloned.1.call-done = bf16[2,2048,512]{2,1,0:T(8,128)(2,1)} async-done(((bf16[2,256,512]{2,1,0:T(8,128)(2,1)}), bf16[2,2048,512]{2,1,0:T(8,128)(2,1)}) %all-gather.8.cloned.1.call-update) | async-done | bytes 4194320 | tf_op jit(solution)/shard_map/all_gather | solution.py:95
  238.5 3.8 add_convert_fusion
  242.6 4.1 convolution_bitcast_fusion
  249.1 6.1 %pad_maximum_fusion = f32[2048,2,1024]{0,2,1:T(8,128)} fusion(f32[2048,1,1024]{0,2,1:T(8,128)S(1)} %convolution_bitcast_fusion, f32[2048,1,1024]{0,2,1:T(8,128)S(1)} %convolution_bitcast_fusion.1), kind=kLoop, calls=%fused_computation.1 | loop fusion | flops 4194304 | bytes 33554432 | tf_op jit(solution)/shard_map/stack | solution.py:129
  255.2 4.3 all-to-all-start
  266.3 8.1 %all-to-all-done = bf16[4,128,512]{2,1,0:T(8,128)(2,1)} async-done(((bf16[4,128,512]{2,1,0:T(8,128)(2,1)}), bf16[4,128,512]{2,1,0:T(8,128)(2,1)}, u32[]{:S(2)}, u32[]{:S(2)}) %all-to-all-start) | async-done | bytes 524320 | tf_op jit(solution)/shard_map/all_to_all | solution.py:80
  277.3 2.9 reshape.95
  284.6 277.1 %reduce-scatter.5.cloned.1.call-done = f32[256,2,1024]{0,2,1:T(8,128)} async-done(((f32[2048,2,1024]{0,2,1:T(8,128)}), f32[256,2,1024]{0,2,1:T(8,128)}) %reduce-scatter.5.cloned.1.call-update) | async-done | bytes 2097168 | tf_op jit(solution)/shard_map/reduce_scatter | solution.py:128
  561.7 5.7 subtract_convert_fusion
  (96 shorter events, 57.2 us)
Async XLA Ops:
  7.2 89.6 %copy-start.18 = (s32[1,128]{1,0:T(1,128)S(1)}, s32[1,128]{1,0:T(1,128)}, u32[]{:S(2)}) copy-start(s32[1,128]{1,0:T(1,128)} %param.11) | copy-start | bytes 1540
  7.2 128.2 %all-gather.4.cloned.1.call-start = ((), (), s32[]{:S(2)}) async-start(), calls=%async_computation.4 | async-start | bytes 4718592 | tf_op jit(solution)/shard_map/all_gather | solution.py:68
  7.9 111.7 %copy-start = (bf16[2,256,512]{2,1,0:T(8,128)(2,1)S(1)}, bf16[2,256,512]{2,1,0:T(8,128)(2,1)}, u32[]{:S(2)}) copy-start(bf16[2,256,512]{2,1,0:T(8,128)(2,1)} %param.14) | copy-start | bytes 1572868
  7.9 150.4 %all-gather.6.cloned.1.call-start = ((), (), s32[]{:S(2)}) async-start(), calls=%async_computation.5 | async-start | bytes 2621440 | tf_op jit(solution)/shard_map/all_gather | solution.py:59
  8.7 224.7 %all-gather.8.cloned.1.call-start = ((), (), s32[]{:S(2)}) async-start(), calls=%async_computation.6 | async-start | bytes 4718592 | tf_op jit(solution)/shard_map/all_gather | solution.py:95
  9.4 19.9 %collective-permute-start = (bf16[2,256,512]{2,1,0:T(8,128)(2,1)}, bf16[2,256,512]{2,1,0:T(8,128)(2,1)S(1)}, u32[]{:S(2)}, u32[]{:S(2)}) collective-permute-start(bf16[2,256,512]{2,1,0:T(8,128)(2,1)} %param.14), channel_id=1, source_target_pairs={{0,4},{4,8},{8,12},{12,16},{16,20},{20,24},{24,28},{28,0},{1,5},{5... | collective-permute-start | bytes 1572872 | tf_op jit(solution)/shard_map/ppermute | solution.py:26
  29.3 26.5 %collective-permute-start.1 = (bf16[2,256,512]{2,1,0:T(8,128)(2,1)S(1)}, bf16[2,256,512]{2,1,0:T(8,128)(2,1)S(1)}, u32[]{:S(2)}, u32[]{:S(2)}) collective-permute-start(bf16[2,256,512]{2,1,0:T(8,128)(2,1)S(1)} %collective-permute-done), channel_id=1, source_target_pairs={{0,4},{4,8},{8,12},{12,16},{16,20},{20,24},{24,28},{28,0},{1,5},{5... | collective-permute-start | bytes 1572872 | tf_op jit(solution)/shard_map/ppermute | solution.py:26
  29.7 26.1 %collective-permute-start.4 = (bf16[2,256,512]{2,1,0:T(8,128)(2,1)}, bf16[2,256,512]{2,1,0:T(8,128)(2,1)S(1)}, u32[]{:S(2)}, u32[]{:S(2)}) collective-permute-start(bf16[2,256,512]{2,1,0:T(8,128)(2,1)} %param.14), channel_id=1, source_target_pairs={{4,0},{8,4},{12,8},{16,12},{20,16},{24,20},{28,24},{0,28},{5,1},{9... | collective-permute-start | bytes 1572872 | tf_op jit(solution)/shard_map/ppermute | solution.py:28
  55.8 31.9 %collective-permute-start.2 = (bf16[2,256,512]{2,1,0:T(8,128)(2,1)S(1)}, bf16[2,256,512]{2,1,0:T(8,128)(2,1)}, u32[]{:S(2)}, u32[]{:S(2)}) collective-permute-start(bf16[2,256,512]{2,1,0:T(8,128)(2,1)S(1)} %collective-permute-done.1), channel_id=1, source_target_pairs={{0,4},{4,8},{8,12},{12,16},{16,20},{20,24},{24,28},{28,0},{1,5},{5... | collective-permute-start | bytes 1572872 | tf_op jit(solution)/shard_map/ppermute | solution.py:26
  55.8 50.1 %collective-permute-start.5 = (bf16[2,256,512]{2,1,0:T(8,128)(2,1)S(1)}, bf16[2,256,512]{2,1,0:T(8,128)(2,1)}, u32[]{:S(2)}, u32[]{:S(2)}) collective-permute-start(bf16[2,256,512]{2,1,0:T(8,128)(2,1)S(1)} %collective-permute-done.4), channel_id=1, source_target_pairs={{4,0},{8,4},{12,8},{16,12},{20,16},{24,20},{28,24},{0,28},{5,1},{9... | collective-permute-start | bytes 1572872 | tf_op jit(solution)/shard_map/ppermute | solution.py:28
  87.7 26.5 %collective-permute-start.3 = (bf16[2,256,512]{2,1,0:T(8,128)(2,1)}, bf16[2,256,512]{2,1,0:T(8,128)(2,1)}, u32[]{:S(2)}, u32[]{:S(2)}) collective-permute-start(bf16[2,256,512]{2,1,0:T(8,128)(2,1)} %collective-permute-done.2), channel_id=1, source_target_pairs={{0,4},{4,8},{8,12},{12,16},{16,20},{20,24},{24,28},{28,0},{1,5},{5... | collective-permute-start | bytes 1572872 | tf_op jit(solution)/shard_map/ppermute | solution.py:26
  92.6 72.7 %all-to-all-start.1 = ((bf16[128,4,512]{2,0,1:T(8,128)(2,1)}), bf16[128,4,512]{2,0,1:T(8,128)(2,1)S(1)}, u32[]{:S(2)}, u32[]{:S(2)}) async-start(bf16[128,4,512]{2,0,1:T(8,128)(2,1)} %copy.19), calls=%async_computation.1 | async-start | bytes 1048576 | tf_op jit(solution)/shard_map/all_to_all | solution.py:84
  96.0 186.4 %reduce-scatter.3.cloned.1.call-start = ((), (), s32[]{:S(2)}) async-start(), calls=%async_computation.7 | async-start | bytes 2621440 | tf_op jit(solution)/shard_map/reduce_scatter | solution.py:110
  105.9 18.2 %collective-permute-start.6 = (bf16[2,256,512]{2,1,0:T(8,128)(2,1)}, bf16[2,256,512]{2,1,0:T(8,128)(2,1)S(1)}, u32[]{:S(2)}, u32[]{:S(2)}) collective-permute-start(bf16[2,256,512]{2,1,0:T(8,128)(2,1)} %collective-permute-done.5), channel_id=1, source_target_pairs={{4,0},{8,4},{12,8},{16,12},{20,16},{24,20},{28,24},{0,28},{5,1},{9... | collective-permute-start | bytes 1572872 | tf_op jit(solution)/shard_map/ppermute | solution.py:28
  139.2 23.8 %copy-start.7 = (bf16[2048,512]{1,0:T(8,128)(2,1)}, bf16[2048,512]{1,0:T(8,128)(2,1)S(1)}, u32[]{:S(2)}) copy-start(bf16[2048,512]{1,0:T(8,128)(2,1)S(1)} %get-tuple-element.27) | copy-start | bytes 6291460
  168.8 67.1 %copy-start.8 = (bf16[2048,512]{1,0:T(8,128)(2,1)S(1)}, bf16[2048,512]{1,0:T(8,128)(2,1)}, u32[]{:S(2)}) copy-start(bf16[2048,512]{1,0:T(8,128)(2,1)} %copy-done.7) | copy-start | bytes 6291460
  242.3 319.4 %reduce-scatter.5.cloned.1.call-start = ((), (), s32[]{:S(2)}) async-start(), calls=%async_computation.8 | async-start | bytes 18874368 | tf_op jit(solution)/shard_map/reduce_scatter | solution.py:128
  255.1 5.4 copy-start.4
  255.1 6.4 %copy-start.15 = (f32[2,256,512]{2,1,0:T(8,128)S(1)}, f32[2,256,512]{2,1,0:T(8,128)}, u32[]{:S(2)}) copy-start(f32[2,256,512]{2,1,0:T(8,128)} %param.17) | copy-start | bytes 3145732
  255.2 6.7 %copy-start.16 = (f32[2,256,512]{2,1,0:T(8,128)S(1)}, f32[2,256,512]{2,1,0:T(8,128)}, u32[]{:S(2)}) copy-start(f32[2,256,512]{2,1,0:T(8,128)} %param.18) | copy-start | bytes 3145732
  255.2 19.3 %all-to-all-start = ((bf16[4,128,512]{2,1,0:T(8,128)(2,1)}), bf16[4,128,512]{2,1,0:T(8,128)(2,1)}, u32[]{:S(2)}, u32[]{:S(2)}) async-start(bf16[4,128,512]{2,1,0:T(8,128)(2,1)} %bitcast.18), calls=%async_computation | async-start | bytes 1048576 | tf_op jit(solution)/shard_map/all_to_all | solution.py:80
  567.3 6.8 %copy-start.3 = (f32[2,256,512]{1,2,0:T(8,128)S(1)}, f32[2,256,512]{1,2,0:T(8,128)}, u32[]{:S(2)}) copy-start(f32[2,256,512]{1,2,0:T(8,128)} %get-tuple-element.31) | copy-start | bytes 3145732
  567.3 8.1 %copy-start.2 = (f32[2,256,512]{1,2,0:T(8,128)S(1)}, f32[2,256,512]{1,2,0:T(8,128)}, u32[]{:S(2)}) copy-start(f32[2,256,512]{1,2,0:T(8,128)} %get-tuple-element.17) | copy-start | bytes 3145732
  567.3 9.4 %copy-start.1 = (f32[2,256,512]{1,2,0:T(8,128)S(1)}, f32[2,256,512]{1,2,0:T(8,128)}, u32[]{:S(2)}) copy-start(f32[2,256,512]{1,2,0:T(8,128)} %get-tuple-element.18) | copy-start | bytes 3145732
  (11 other events, 34.0 us)
Sparse Core Ops, SparseCore 0:
  10.2 125.1 all-gather.3
  136.9 21.3 all-gather.5
  160.5 72.7 all-gather.7
  242.4 35.3 reduce-scatter.2
  281.4 280.2 reduce-scatter.4
